TPU v7x, 512 devices: a whole 4x4x16 slice. The times are simulated.
512 devices in a mesh: row: 16 (over x, y), col: 32 (over z, core).
Axes of the slice: x: 4, y: 4, z: 16, core: 2. Of those that a mesh axis runs over, the one named last changes fastest.
Arguments:
- rhs: float32 [36864, 128], P('row'), may hold values from -6 to 6
- factor: float32 [34816, 4096], P('row', 'col'), may hold values from -0.09375 to 0.09375
- inverses: float32 [2, 2048, 2048], P(None, 'col', 'row'), may hold values from -1 to 3, as said below
Outputs:
- solution: float32 [4096, 128], P('col')
- remaining: float32 [32768, 128], P('row')
Inputs may be any that keep to these rules, and one draw needn't show every extreme that they name: Each inverses[k] is lower triangular in panel order with positive diagonal entries.
All inputs are finite; a program needn't handle non-finite values.
Results may differ from a plain program's by a relative error of at most 0.000068.
Values sent between devices are 32-bit elements; how exact they have to be, the bound alone decides.
No kernel may reach another device: no remote copies, remote signals or barrier semaphores. Data moves between devices by JAX's collectives and lax.ppermute only.
A program may use at most 64 MiB of HBM per device.

v0:
```python
import jax
import jax.numpy as jnp
from jax import lax
from jax.experimental.layout import Layout, with_layout_constraint
from jax.sharding import Mesh
from jax.sharding import PartitionSpec as P

ROW = ("x", "y")
NEAR = ("pair", "core")
Z = ("parity", "pair")
COL = (*Z, "core")
SWAP = [(0, 1), (1, 0)]


def exchanged(blocks, axis):
    return lax.all_to_all(blocks, axis, split_axis=0, concat_axis=0, tiled=True)


def from_everyone(array, axis):
    return exchanged(jnp.broadcast_to(array, (lax.axis_size(axis), *array.shape)), axis)


def taken_together(array, axis):
    return jnp.sum(from_everyone(array, axis), axis=0)


def my_sum(array, axis):
    count = lax.axis_size(axis)
    blocks = array.reshape(count, array.shape[0] // count, *array.shape[1:])
    return jnp.sum(exchanged(blocks, axis), axis=0)


def product(left, right, precision=lax.Precision.HIGHEST):
    return jnp.dot(left, right, precision=precision, preferred_element_type=jnp.float32)


def part_of(array, start, rows):
    return lax.dynamic_slice(
        array, (start, 0), (rows, array.shape[1]), allow_negative_indices=False
    )


def quarter_of(blocks, first, pair):
    sizes = (blocks.shape[0] // 2, 1, *blocks.shape[2:])
    part = lax.dynamic_slice(blocks, (first, pair, 0, 0), sizes, allow_negative_indices=False)
    return part.reshape(-1, blocks.shape[-1])


def local(rhs, factor, inverses):
    span_rows = inverses.shape[2]
    span_cols = factor.shape[1] // 2
    first_rhs = rhs[:span_rows]
    second_rhs = rhs[span_rows : 2 * span_rows]
    spots = lax.axis_size(Z)
    rows = (rhs.shape[0] - 2 * span_rows) // (2 * spots)
    half = spots * rows
    side = lax.axis_index("core") ^ lax.axis_index("pair")
    pair = lax.axis_index("pair")
    place = 2 * span_rows + side * half + lax.axis_index(Z) * rows
    near_rows = span_rows // lax.axis_size(NEAR)
    near = lax.axis_index(NEAR) * near_rows
    core, other_core = (lax.axis_index("core"), 1 - lax.axis_index("core"))
    other_pair, group = (1 - pair, spots // 2)
    unknowns = factor.shape[1]
    starts = (
        1 + side * group,
        1 + (1 - side) * group,
        pair,
        other_pair,
        near,
        place,
        (pair * 2 + other_core) * unknowns,
        (other_pair * 2 + other_core) * unknowns,
        (other_pair * 2 + core) * unknowns,
    )
    first_part = product(inverses[0], first_rhs)
    first_part, second_rhs, starts = lax.optimization_barrier((first_part, second_rhs, starts))
    blocks_at, other_at, pair, other_pair, near, place, across_at, crossed_at, straight_at = starts
    first_sol = taken_together(first_part, ROW)
    coupled = lax.optimization_barrier(product(factor[:span_rows, :span_cols], first_sol))
    coupled = with_layout_constraint(coupled, Layout((0, 1)))
    coupled = lax.all_gather(coupled, NEAR, axis=0)
    coupled = lax.dynamic_slice(
        coupled,
        (0, near, 0),
        (coupled.shape[0], near_rows, coupled.shape[2]),
        allow_negative_indices=False,
    )
    coupled = jnp.sum(coupled, axis=0)
    coupled = lax.all_gather(taken_together(coupled, "parity"), NEAR, axis=0, tiled=True)
    second_part = product(inverses[1], second_rhs - coupled)
    second_part, factor, rhs = lax.optimization_barrier((second_part, factor, rhs))
    blocks = factor.reshape(-1, 2, rows, factor.shape[1])
    own = quarter_of(blocks, blocks_at, pair)
    across = quarter_of(blocks, other_at, pair)
    crossed = quarter_of(blocks, blocks_at, other_pair)
    straight = quarter_of(blocks, other_at, other_pair)
    across = lax.ppermute(across, NEAR, [(0, 1), (1, 0), (2, 3), (3, 2)])
    crossed = lax.ppermute(crossed, NEAR, [(0, 3), (3, 0), (1, 2), (2, 1)])
    straight = lax.ppermute(straight, NEAR, [(0, 2), (2, 0), (1, 3), (3, 1)])
    trailing = part_of(rhs, place, rows)
    second_sol = taken_together(second_part, ROW)
    second_sol, own, trailing = lax.optimization_barrier((second_sol, own, trailing))
    both = lax.optimization_barrier(jnp.concatenate([first_sol, second_sol], 0))
    near_both = lax.all_gather(both, NEAR, axis=0, tiled=True)
    theirs = [part_of(near_both, at, both.shape[0]) for at in (across_at, crossed_at, straight_at)]
    columns = jnp.concatenate([own, across, crossed, straight], 1)
    terms = product(columns, jnp.concatenate([both, *theirs], 0), lax.Precision.HIGH)
    terms = my_sum(with_layout_constraint(terms, Layout((0, 1))), "parity")
    rings = [[2 * z + (z + start) % 2 for z in range(spots)] for start in range(2)]
    mine = lax.all_gather(trailing - terms, COL, axis=0, tiled=True, axis_index_groups=rings)
    other = lax.ppermute(mine, "core", SWAP)
    remaining = jnp.where(
        side == 0, jnp.concatenate([mine, other], 0), jnp.concatenate([other, mine], 0)
    )
    return (both, remaining)


def solution(mesh):
    rows, cols = mesh.devices.shape
    shape = (4, rows // 4, cols // 4, 2, 2)
    torus = Mesh(mesh.devices.reshape(shape), (*ROW, *COL))
    in_specs = (P(ROW, None), P(ROW, COL), P(None, COL, ROW))
    out_specs = (P(COL, None), P(ROW, None))
    return jax.shard_map(local, mesh=torus, in_specs=in_specs, out_specs=out_specs, check_vma=False)
```

profile of v0, /device:TPU:1, one launch (start us, length us, event | category | flops | bytes accessed | tf_op | source)
XLA Modules:
  0.0 142.8 jit_solution(4184857471511900030)
XLA Ops:
  0.7 0.0 copy-start
  0.7 1.1 fusion.17
  1.9 0.0 slice-start
  1.9 0.0 copy-start.3
  1.9 16.7 %all_to_all.20 = f32[16,64,128]{2,1,0:T(8,128)S(1)} all-to-all(f32[16,64,128]{2,1,0:T(8,128)S(1)} %broadcast_in_dim.9), channel_id=1, replica_groups=mesh['x'=4,'y'=4,'parity'=8,'pair'=2,'core'=2] {'x','y'}, dimensions={0} | all-to-all | bytes 1048576 | tf_op jit(solution)/shard_map/all_to_all | solution.py:16
  18.6 0.0 copy-done
  18.7 0.2 convolution_bitcast_fusion
  18.9 9.2 %all-gather = f32[512,128]{1,0:T(8,128)S(1)} all-gather(f32[128,128]{1,0:T(8,128)S(1)} %convolution_bitcast_fusion), channel_id=2, replica_groups=mesh['x'=4,'y'=4,'parity'=8,'pair'=2,'core'=2] {'pair','core'}, dimensions={0}, use_global_device_ids=true | all-gather | bytes 327680 | tf_op jit(solution)/shard_map/all_gather | solution.py:82
  28.1 27.8 %all_to_all.21 = f32[8,32,128]{2,1,0:T(8,128)S(1)} all-to-all(f32[8,32,128]{2,1,0:T(8,128)S(1)} %broadcast_in_dim.10), channel_id=1, replica_groups=mesh['x'=4,'y'=4,'parity'=8,'pair'=2,'core'=2] {'parity'}, dimensions={0} | all-to-all | bytes 262144 | tf_op jit(solution)/shard_map/all_to_all | solution.py:16
  55.9 8.4 %all_gather.17 = f32[128,128]{1,0:T(8,128)S(1)} all-gather(f32[32,128]{1,0:T(8,128)S(1)} %reduce_sum.47), channel_id=1, replica_groups=mesh['x'=4,'y'=4,'parity'=8,'pair'=2,'core'=2] {'pair','core'}, dimensions={0}, use_global_device_ids=true | all-gather | bytes 81920 | tf_op jit(solution)/shard_map/all_gather | solution.py:90
  64.4 0.0 slice-done
  64.4 0.0 copy-done.3
  64.4 0.2 convolution_bitcast_fusion.1
  64.6 0.8 broadcast_in_dim.11
  65.4 3.6 %all-to-all-start.2 = ((f32[16,64,128]{2,1,0:T(8,128)}), f32[16,64,128]{2,1,0:T(8,128)S(1)}, u32[]{:S(2)}, u32[]{:S(2)}) async-start(f32[16,64,128]{2,1,0:T(8,128)} %broadcast_in_dim.11), calls=%async_computation.2 | async-start | bytes 1048576 | tf_op jit(solution)/shard_map/all_to_all | solution.py:16
  69.0 0.0 copy-start.2
  69.0 0.1 constant_dynamic-slice_fusion.5
  69.1 2.4 %collective-permute-start.2 = (f32[512,128]{1,0:T(8,128)S(1)}, f32[512,128]{1,0:T(8,128)S(1)}, u32[]{:S(2)}, u32[]{:S(2)}) collective-permute-start(f32[512,128]{1,0:T(8,128)S(1)} %bitcast.23), channel_id=1, source_target_pairs={{0,2},{2,0},{1,3},{3,1},{4,6},{6,4},{5,7},{7,5},{8,10},{10,8},{9,1... | collective-permute-start | bytes 786440 | tf_op jit(solution)/shard_map/ppermute | solution.py:100
  71.6 2.4 %collective-permute-start = (f32[512,128]{1,0:T(8,128)S(1)}, f32[512,128]{1,0:T(8,128)S(1)}, u32[]{:S(2)}, u32[]{:S(2)}) collective-permute-start(f32[512,128]{1,0:T(8,128)S(1)} %bitcast.22), channel_id=1, source_target_pairs={{0,1},{1,0},{2,3},{3,2},{4,5},{5,4},{6,7},{7,6},{8,9},{9,8},{10,11... | collective-permute-start | bytes 786440 | tf_op jit(solution)/shard_map/ppermute | solution.py:98
  73.9 3.0 %collective-permute-start.1 = (f32[512,128]{1,0:T(8,128)S(1)}, f32[512,128]{1,0:T(8,128)S(1)}, u32[]{:S(2)}, u32[]{:S(2)}) collective-permute-start(f32[512,128]{1,0:T(8,128)S(1)} %bitcast.21), channel_id=1, source_target_pairs={{0,3},{3,0},{1,2},{2,1},{4,7},{7,4},{5,6},{6,5},{8,11},{11,8},{9,1... | collective-permute-start | bytes 786440 | tf_op jit(solution)/shard_map/ppermute | solution.py:99
  76.9 0.0 copy-done.2
  76.9 2.6 %all-to-all-done.2 = f32[16,64,128]{2,1,0:T(8,128)S(1)} async-done(((f32[16,64,128]{2,1,0:T(8,128)}), f32[16,64,128]{2,1,0:T(8,128)S(1)}, u32[]{:S(2)}, u32[]{:S(2)}) %all-to-all-start.2) | async-done | bytes 524320 | tf_op jit(solution)/shard_map/all_to_all | solution.py:16
  79.5 0.0 copy-start.1
  79.5 8.0 %all_gather.18 = f32[512,128]{1,0:T(8,128)S(1)} all-gather(f32[128,128]{1,0:T(8,128)S(1)} %pad_maximum_fusion), channel_id=1, replica_groups=mesh['x'=4,'y'=4,'parity'=8,'pair'=2,'core'=2] {'pair','core'}, dimensions={0}, use_global_device_ids=true | all-gather | bytes 327680 | tf_op jit(solution)/shard_map/all_gather | solution.py:105
  87.6 0.0 collective-permute-done.2
  87.6 0.0 collective-permute-done
  87.6 0.0 collective-permute-done.1
  87.6 0.6 fusion
  88.2 0.0 copy-done.1
  88.3 23.8 %all_to_all.22 = f32[8,64,128]{2,1,0:T(8,128)S(1)} all-to-all(f32[8,64,128]{2,1,0:T(8,128)S(1)} %bitcast.24), channel_id=1, replica_groups=mesh['x'=4,'y'=4,'parity'=8,'pair'=2,'core'=2] {'parity'}, dimensions={0} | all-to-all | bytes 524288 | tf_op jit(solution)/shard_map/all_to_all | solution.py:16
  112.1 25.8 %all_gather.19 = f32[1024,128]{1,0:T(8,128)S(1)} all-gather(f32[64,128]{1,0:T(8,128)S(1)} %sub.19), channel_id=1, replica_groups={{0,3,4,7,8,11,12,15,16,19,20,23,24,27,28,31},{1,2,5,6,9,10,13,14,17,18,..., dimensions={0}, use_global_device_ids=true | all-gather | bytes 557056 | tf_op jit(solution)/shard_map/all_gather | solution.py:111
  137.9 2.2 %collective-permute-start.3 = (f32[1024,128]{1,0:T(8,128)S(1)}, f32[1024,128]{1,0:T(8,128)S(1)}, u32[]{:S(2)}, u32[]{:S(2)}) collective-permute-start(f32[1024,128]{1,0:T(8,128)S(1)} %all_gather.19), channel_id=1, source_target_pairs={{0,1},{1,0},{2,3},{3,2},{4,5},{5,4},{6,7},{7,6},{8,9},{9,8},{10,11... | collective-permute-start | bytes 1572872 | tf_op jit(solution)/shard_map/ppermute | solution.py:112
  140.1 1.6 %collective-permute-done.3 = f32[1024,128]{1,0:T(8,128)S(1)} collective-permute-done((f32[1024,128]{1,0:T(8,128)S(1)}, f32[1024,128]{1,0:T(8,128)S(1)}, u32[]{:S(2)}, u32[]{:S(2)}) %collective-permute-start.3) | collective-permute-done | bytes 524320 | tf_op jit(solution)/shard_map/ppermute | solution.py:112
  141.7 1.1 maximum_select_fusion
  (11 shorter events, 0.2 us)
Async XLA Ops:
  0.7 18.0 %copy-start = (f32[2176,128]{1,0:T(8,128)S(1)}, f32[2176,128]{1,0:T(8,128)}, u32[]{:S(2)}) copy-start(f32[2176,128]{1,0:T(8,128)} %param.4) | copy-start | bytes 3342340
  1.9 62.5 %slice-start = ((f32[2304,128]{1,0:T(8,128)}), f32[128,128]{1,0:T(8,128)S(1)}, s32[]{:S(2)}) async-start(f32[2304,128]{1,0:T(8,128)} %param.3), calls=%async_computation.4 | async-start | bytes 131072 | tf_op jit(solution)/shard_map/slice | solution.py:53
  1.9 62.5 %copy-start.3 = (f32[2,64,128]{2,1,0:T(8,128)S(1)}, f32[2,64,128]{2,1,0:T(8,128)}, u32[]{:S(2)}) copy-start(f32[2,64,128]{2,1,0:T(8,128)} %param.5) | copy-start | bytes 196612
  65.4 14.1 %all-to-all-start.2 = ((f32[16,64,128]{2,1,0:T(8,128)}), f32[16,64,128]{2,1,0:T(8,128)S(1)}, u32[]{:S(2)}, u32[]{:S(2)}) async-start(f32[16,64,128]{2,1,0:T(8,128)} %broadcast_in_dim.11), calls=%async_computation.2 | async-start | bytes 1048576 | tf_op jit(solution)/shard_map/all_to_all | solution.py:16
  69.0 7.9 %copy-start.2 = (f32[2304,128]{1,0:T(8,128)S(1)}, f32[2304,128]{1,0:T(8,128)}, u32[]{:S(2)}) copy-start(f32[2304,128]{1,0:T(8,128)} %param.3) | copy-start | bytes 3538948
  69.1 18.5 %collective-permute-start.2 = (f32[512,128]{1,0:T(8,128)S(1)}, f32[512,128]{1,0:T(8,128)S(1)}, u32[]{:S(2)}, u32[]{:S(2)}) collective-permute-start(f32[512,128]{1,0:T(8,128)S(1)} %bitcast.23), channel_id=1, source_target_pairs={{0,2},{2,0},{1,3},{3,1},{4,6},{6,4},{5,7},{7,5},{8,10},{10,8},{9,1... | collective-permute-start | bytes 786440 | tf_op jit(solution)/shard_map/ppermute | solution.py:100
  71.6 16.1 %collective-permute-start = (f32[512,128]{1,0:T(8,128)S(1)}, f32[512,128]{1,0:T(8,128)S(1)}, u32[]{:S(2)}, u32[]{:S(2)}) collective-permute-start(f32[512,128]{1,0:T(8,128)S(1)} %bitcast.22), channel_id=1, source_target_pairs={{0,1},{1,0},{2,3},{3,2},{4,5},{5,4},{6,7},{7,6},{8,9},{9,8},{10,11... | collective-permute-start | bytes 786440 | tf_op jit(solution)/shard_map/ppermute | solution.py:98
  73.9 13.7 %collective-permute-start.1 = (f32[512,128]{1,0:T(8,128)S(1)}, f32[512,128]{1,0:T(8,128)S(1)}, u32[]{:S(2)}, u32[]{:S(2)}) collective-permute-start(f32[512,128]{1,0:T(8,128)S(1)} %bitcast.21), channel_id=1, source_target_pairs={{0,3},{3,0},{1,2},{2,1},{4,7},{7,4},{5,6},{6,5},{8,11},{11,8},{9,1... | collective-permute-start | bytes 786440 | tf_op jit(solution)/shard_map/ppermute | solution.py:99
  79.5 8.7 %copy-start.1 = (f32[128,128]{1,0:T(8,128)}, f32[128,128]{1,0:T(8,128)S(1)}, u32[]{:S(2)}) copy-start(f32[128,128]{1,0:T(8,128)S(1)} %pad_maximum_fusion) | copy-start | bytes 196612
  137.9 3.8 %collective-permute-start.3 = (f32[1024,128]{1,0:T(8,128)S(1)}, f32[1024,128]{1,0:T(8,128)S(1)}, u32[]{:S(2)}, u32[]{:S(2)}) collective-permute-start(f32[1024,128]{1,0:T(8,128)S(1)} %all_gather.19), channel_id=1, source_target_pairs={{0,1},{1,0},{2,3},{3,2},{4,5},{5,4},{6,7},{7,6},{8,9},{9,8},{10,11... | collective-permute-start | bytes 1572872 | tf_op jit(solution)/shard_map/ppermute | solution.py:112
where the time goes:
time: 143 us
  blocking collectives  120 us (84%)
  starting transfers between devices  13.5 us (9%)
  waiting for transfers between devices  4.16 us (3%)
  matrix products  2.11 us (1%)
    all_to_all x3, blocking collectives, exchanged(): return lax.all_to_all(blocks, axis, split_axis=0, concat_axis=0, tiled=True)  68.3 us
    all_gather x1, blocking collectives, local(): lax.all_gather(trailing - terms, COL, axis=0, tiled=True, axis_index_grou...  25.8 us
    all_gather x1, blocking collectives, local(): coupled = lax.all_gather(coupled, NEAR, axis=0)  9.24 us
    all_gather x1, blocking collectives, local(): lax.all_gather(taken_together(coupled, 'parity'), NEAR, axis=0, tiled=True)  8.44 us
    all_gather x1, blocking collectives, local(): near_both = lax.all_gather(both, NEAR, axis=0, tiled=True)  8.04 us
    all_to_all x1, starting transfers between devices, exchanged(): return lax.all_to_all(blocks, axis, split_axis=0, concat_axis=0, tiled=True)  3.57 us
    ppermute x1, starting transfers between devices, local(): crossed = lax.ppermute(crossed, NEAR, [(0, 3), (3, 0), (1, 2), (2, 1)])  2.95 us
  transfers between devices with their start and end apart: 5, of which 2 were waited for; matrix products, arithmetic and copies ran while one was open for 0% of the time, Pallas kernels for 0%

commit v1 on v0

--- a/solution.py
+++ b/solution.py
@@ -1,15 +1,27 @@
+import functools
 import jax
 import jax.numpy as jnp
 from jax import lax
 from jax.experimental.layout import Layout, with_layout_constraint
 from jax.sharding import Mesh
 from jax.sharding import PartitionSpec as P
+from jax.lax import all_to_all, axis_size
 
 ROW = ("x", "y")
 NEAR = ("pair", "core")
 Z = ("parity", "pair")
 COL = (*Z, "core")
 SWAP = [(0, 1), (1, 0)]
+
+
+def direct_scenes(inp, axis_name):
+    response = axis_size(axis_name)
+    y2 = jnp.stack([inp] * response, axis=0)
+    fresh = all_to_all(y2, axis_name, 0, 0)
+    return jnp.concatenate(fresh, 0)
+
+
+_obtain_shelves = functools.partial(direct_scenes, axis_name=NEAR)
 
 
 def exchanged(blocks, axis):
@@ -102,7 +114,7 @@
     second_sol = taken_together(second_part, ROW)
     second_sol, own, trailing = lax.optimization_barrier((second_sol, own, trailing))
     both = lax.optimization_barrier(jnp.concatenate([first_sol, second_sol], 0))
-    near_both = lax.all_gather(both, NEAR, axis=0, tiled=True)
+    near_both = _obtain_shelves(both)
     theirs = [part_of(near_both, at, both.shape[0]) for at in (across_at, crossed_at, straight_at)]
     columns = jnp.concatenate([own, across, crossed, straight], 1)
     terms = product(columns, jnp.concatenate([both, *theirs], 0), lax.Precision.HIGH)

time: 143 us -> 158 us (1.10)
  waiting for transfers between devices: 4.16 us -> 20.6 us
  blocking collectives: 120 us -> 112 us
  starting transfers between devices: 13.5 us -> 19.1 us
    all_gather x1 -> x0, blocking collectives: 8.04 us -> none  [local(): near_both = lax.all_gather(both, NEAR, axis=0, tiled=True)]
    all_to_all x1, waiting for transfers between devices: 2.57 us -> 10.3 us  [exchanged(): return lax.all_to_all(blocks, axis, split_axis=0, concat_axis=0, tiled=True)]
    ppermute x1, waiting for transfers between devices: 0.01 us -> 5.8 us  [local(): crossed = lax.ppermute(crossed, NEAR, [(0, 3), (3, 0), (1, 2), (2, 1)])]
    all_to_all x0 -> x1, starting transfers between devices: none -> 5.3 us  [direct_scenes(): fresh = all_to_all(y2, axis_name, 0, 0)]
    ppermute x1, waiting for transfers between devices: 0.01 us -> 2.96 us  [local(): straight = lax.ppermute(straight, NEAR, [(0, 2), (2, 0), (1, 3), (3, 1)])]
  transfers between devices with their start and end apart: 5 -> 6, of which waited for: 2 -> 4; matrix products, arithmetic and copies ran while one was open for 0% -> 0% of each run, Pallas kernels for 0% -> 0%
where the time goes in v1:
time: 158 us; the launch traced here: 157 us
  blocking collectives  112 us (71%)
  waiting for transfers between devices  20.6 us (13%)
  starting transfers between devices  19.1 us (12%)
  matrix products  2.1 us (1%)
  local copies, waits for them, and re-layouts  1.81 us (1%)
    all_to_all x3, blocking collectives, exchanged(): return lax.all_to_all(blocks, axis, split_axis=0, concat_axis=0, tiled=True)  68.5 us
    all_gather x1, blocking collectives, local(): lax.all_gather(trailing - terms, COL, axis=0, tiled=True, axis_index_grou...  25.4 us
    all_to_all x1, waiting for transfers between devices, exchanged(): return lax.all_to_all(blocks, axis, split_axis=0, concat_axis=0, tiled=True)  10.3 us
    all_gather x1, blocking collectives, local(): coupled = lax.all_gather(coupled, NEAR, axis=0)  9.24 us
    all_gather x1, blocking collectives, local(): lax.all_gather(taken_together(coupled, 'parity'), NEAR, axis=0, tiled=True)  8.44 us
    ppermute x1, waiting for transfers between devices, local(): crossed = lax.ppermute(crossed, NEAR, [(0, 3), (3, 0), (1, 2), (2, 1)])  5.8 us
    all_to_all x1, starting transfers between devices, direct_scenes(): fresh = all_to_all(y2, axis_name, 0, 0)  5.3 us
    all_to_all x1, starting transfers between devices, exchanged(): return lax.all_to_all(blocks, axis, split_axis=0, concat_axis=0, tiled=True)  3.57 us
  transfers between devices with their start and end apart: 6, of which 4 were waited for; matrix products, arithmetic and copies ran while one was open for 0% of the time, Pallas kernels for 0%

profile of v1, /device:TPU:1, one launch (start us, length us, event | category | flops | bytes accessed | tf_op | source)
XLA Modules:
  0.0 157.2 jit_solution(1876692744442292571)
XLA Ops:
  0.7 0.0 copy-start
  0.7 1.1 fusion.17
  1.9 0.0 slice-start
  1.9 0.0 copy-start.3
  1.9 16.7 %all_to_all.25 = f32[16,64,128]{2,1,0:T(8,128)S(1)} all-to-all(f32[16,64,128]{2,1,0:T(8,128)S(1)} %broadcast_in_dim.9), channel_id=1, replica_groups=mesh['x'=4,'y'=4,'parity'=8,'pair'=2,'core'=2] {'x','y'}, dimensions={0} | all-to-all | bytes 1048576 | tf_op jit(solution)/shard_map/all_to_all | solution.py:28
  18.6 0.0 copy-done
  18.7 0.2 convolution_bitcast_fusion
  18.9 9.2 %all-gather = f32[512,128]{1,0:T(8,128)S(1)} all-gather(f32[128,128]{1,0:T(8,128)S(1)} %convolution_bitcast_fusion), channel_id=2, replica_groups=mesh['x'=4,'y'=4,'parity'=8,'pair'=2,'core'=2] {'pair','core'}, dimensions={0}, use_global_device_ids=true | all-gather | bytes 327680 | tf_op jit(solution)/shard_map/all_gather | solution.py:94
  28.1 0.0 copy-start.2
  28.1 27.9 %all_to_all.26 = f32[8,32,128]{2,1,0:T(8,128)S(1)} all-to-all(f32[8,32,128]{2,1,0:T(8,128)S(1)} %broadcast_in_dim.10), channel_id=1, replica_groups=mesh['x'=4,'y'=4,'parity'=8,'pair'=2,'core'=2] {'parity'}, dimensions={0} | all-to-all | bytes 262144 | tf_op jit(solution)/shard_map/all_to_all | solution.py:28
  56.1 8.4 %all_gather.14 = f32[128,128]{1,0:T(8,128)S(1)} all-gather(f32[32,128]{1,0:T(8,128)S(1)} %reduce_sum.47), channel_id=1, replica_groups=mesh['x'=4,'y'=4,'parity'=8,'pair'=2,'core'=2] {'pair','core'}, dimensions={0}, use_global_device_ids=true | all-gather | bytes 81920 | tf_op jit(solution)/shard_map/all_gather | solution.py:102
  64.5 0.0 slice-done
  64.5 0.0 copy-done.3
  64.5 0.2 convolution_bitcast_fusion.1
  64.7 0.8 broadcast_in_dim.11
  65.6 3.6 %all-to-all-start.2 = ((f32[16,64,128]{2,1,0:T(8,128)}), f32[16,64,128]{2,1,0:T(8,128)S(1)}, u32[]{:S(2)}, u32[]{:S(2)}) async-start(f32[16,64,128]{2,1,0:T(8,128)} %broadcast_in_dim.11), calls=%async_computation.2 | async-start | bytes 1048576 | tf_op jit(solution)/shard_map/all_to_all | solution.py:28
  69.2 0.0 copy-done.2
  69.2 0.1 constant_dynamic-slice_fusion.5
  69.3 10.3 %all-to-all-done.2 = f32[16,64,128]{2,1,0:T(8,128)S(1)} async-done(((f32[16,64,128]{2,1,0:T(8,128)}), f32[16,64,128]{2,1,0:T(8,128)S(1)}, u32[]{:S(2)}, u32[]{:S(2)}) %all-to-all-start.2) | async-done | bytes 524320 | tf_op jit(solution)/shard_map/all_to_all | solution.py:28
  79.7 0.0 copy-start.1
  79.7 0.7 stack.2
  80.4 5.3 %all-to-all-start.3 = ((f32[4,128,128]{2,1,0:T(8,128)}), f32[4,128,128]{2,1,0:T(8,128)S(1)}, u32[]{:S(2)}, u32[]{:S(2)}) async-start(f32[4,128,128]{2,1,0:T(8,128)} %stack.2), calls=%async_computation.3 | async-start | bytes 524288 | tf_op jit(solution)/shard_map/all_to_all | solution.py:20
  85.7 3.3 %collective-permute-start.2 = (f32[512,128]{1,0:T(8,128)S(1)}, f32[512,128]{1,0:T(8,128)S(1)}, u32[]{:S(2)}, u32[]{:S(2)}) collective-permute-start(f32[512,128]{1,0:T(8,128)S(1)} %bitcast.25), channel_id=1, source_target_pairs={{0,2},{2,0},{1,3},{3,1},{4,6},{6,4},{5,7},{7,5},{8,10},{10,8},{9,1... | collective-permute-start | bytes 786440 | tf_op jit(solution)/shard_map/ppermute | solution.py:112
  89.0 2.5 %collective-permute-start = (f32[512,128]{1,0:T(8,128)S(1)}, f32[512,128]{1,0:T(8,128)S(1)}, u32[]{:S(2)}, u32[]{:S(2)}) collective-permute-start(f32[512,128]{1,0:T(8,128)S(1)} %bitcast.24), channel_id=1, source_target_pairs={{0,1},{1,0},{2,3},{3,2},{4,5},{5,4},{6,7},{7,6},{8,9},{9,8},{10,11... | collective-permute-start | bytes 786440 | tf_op jit(solution)/shard_map/ppermute | solution.py:110
  91.6 1.9 %collective-permute-start.1 = (f32[512,128]{1,0:T(8,128)S(1)}, f32[512,128]{1,0:T(8,128)S(1)}, u32[]{:S(2)}, u32[]{:S(2)}) collective-permute-start(f32[512,128]{1,0:T(8,128)S(1)} %bitcast.23), channel_id=1, source_target_pairs={{0,3},{3,0},{1,2},{2,1},{4,7},{7,4},{5,6},{6,5},{8,11},{11,8},{9,1... | collective-permute-start | bytes 786440 | tf_op jit(solution)/shard_map/ppermute | solution.py:111
  93.5 0.0 all-to-all-done.3
  93.5 3.0 %collective-permute-done.2 = f32[512,128]{1,0:T(8,128)S(1)} collective-permute-done((f32[512,128]{1,0:T(8,128)S(1)}, f32[512,128]{1,0:T(8,128)S(1)}, u32[]{:S(2)}, u32[]{:S(2)}) %collective-permute-start.2) | collective-permute-done | bytes 262176 | tf_op jit(solution)/shard_map/ppermute | solution.py:112
  96.5 0.0 collective-permute-done
  96.5 5.8 %collective-permute-done.1 = f32[512,128]{1,0:T(8,128)S(1)} collective-permute-done((f32[512,128]{1,0:T(8,128)S(1)}, f32[512,128]{1,0:T(8,128)S(1)}, u32[]{:S(2)}, u32[]{:S(2)}) %collective-permute-start.1) | collective-permute-done | bytes 262176 | tf_op jit(solution)/shard_map/ppermute | solution.py:111
  102.3 0.6 fusion
  102.9 0.0 copy-done.1
  102.9 23.8 %all_to_all.27 = f32[8,64,128]{2,1,0:T(8,128)S(1)} all-to-all(f32[8,64,128]{2,1,0:T(8,128)S(1)} %bitcast.26), channel_id=1, replica_groups=mesh['x'=4,'y'=4,'parity'=8,'pair'=2,'core'=2] {'parity'}, dimensions={0} | all-to-all | bytes 524288 | tf_op jit(solution)/shard_map/all_to_all | solution.py:28
  126.8 25.4 %all_gather.15 = f32[1024,128]{1,0:T(8,128)S(1)} all-gather(f32[64,128]{1,0:T(8,128)S(1)} %sub.19), channel_id=1, replica_groups={{0,3,4,7,8,11,12,15,16,19,20,23,24,27,28,31},{1,2,5,6,9,10,13,14,17,18,..., dimensions={0}, use_global_device_ids=true | all-gather | bytes 557056 | tf_op jit(solution)/shard_map/all_gather | solution.py:123
  152.1 2.5 %collective-permute-start.3 = (f32[1024,128]{1,0:T(8,128)S(1)}, f32[1024,128]{1,0:T(8,128)S(1)}, u32[]{:S(2)}, u32[]{:S(2)}) collective-permute-start(f32[1024,128]{1,0:T(8,128)S(1)} %all_gather.15), channel_id=1, source_target_pairs={{0,1},{1,0},{2,3},{3,2},{4,5},{5,4},{6,7},{7,6},{8,9},{9,8},{10,11... | collective-permute-start | bytes 1572872 | tf_op jit(solution)/shard_map/ppermute | solution.py:124
  154.6 1.5 collective-permute-done.3
  156.1 1.1 maximum_select_fusion
  (11 shorter events, 0.2 us)
Async XLA Ops:
  0.7 18.0 %copy-start = (f32[2176,128]{1,0:T(8,128)S(1)}, f32[2176,128]{1,0:T(8,128)}, u32[]{:S(2)}) copy-start(f32[2176,128]{1,0:T(8,128)} %param.4) | copy-start | bytes 3342340
  1.9 62.7 %slice-start = ((f32[2304,128]{1,0:T(8,128)}), f32[128,128]{1,0:T(8,128)S(1)}, s32[]{:S(2)}) async-start(f32[2304,128]{1,0:T(8,128)} %param.3), calls=%async_computation.5 | async-start | bytes 131072 | tf_op jit(solution)/shard_map/slice | solution.py:65
  1.9 62.7 %copy-start.3 = (f32[2,64,128]{2,1,0:T(8,128)S(1)}, f32[2,64,128]{2,1,0:T(8,128)}, u32[]{:S(2)}) copy-start(f32[2,64,128]{2,1,0:T(8,128)} %param.5) | copy-start | bytes 196612
  28.1 41.0 %copy-start.2 = (f32[2304,128]{1,0:T(8,128)S(1)}, f32[2304,128]{1,0:T(8,128)}, u32[]{:S(2)}) copy-start(f32[2304,128]{1,0:T(8,128)} %param.3) | copy-start | bytes 3538948
  65.6 14.1 %all-to-all-start.2 = ((f32[16,64,128]{2,1,0:T(8,128)}), f32[16,64,128]{2,1,0:T(8,128)S(1)}, u32[]{:S(2)}, u32[]{:S(2)}) async-start(f32[16,64,128]{2,1,0:T(8,128)} %broadcast_in_dim.11), calls=%async_computation.2 | async-start | bytes 1048576 | tf_op jit(solution)/shard_map/all_to_all | solution.py:28
  79.7 23.2 %copy-start.1 = (f32[128,128]{1,0:T(8,128)}, f32[128,128]{1,0:T(8,128)S(1)}, u32[]{:S(2)}) copy-start(f32[128,128]{1,0:T(8,128)S(1)} %pad_maximum_fusion) | copy-start | bytes 196612
  80.4 13.1 %all-to-all-start.3 = ((f32[4,128,128]{2,1,0:T(8,128)}), f32[4,128,128]{2,1,0:T(8,128)S(1)}, u32[]{:S(2)}, u32[]{:S(2)}) async-start(f32[4,128,128]{2,1,0:T(8,128)} %stack.2), calls=%async_computation.3 | async-start | bytes 524288 | tf_op jit(solution)/shard_map/all_to_all | solution.py:20
  85.7 10.8 %collective-permute-start.2 = (f32[512,128]{1,0:T(8,128)S(1)}, f32[512,128]{1,0:T(8,128)S(1)}, u32[]{:S(2)}, u32[]{:S(2)}) collective-permute-start(f32[512,128]{1,0:T(8,128)S(1)} %bitcast.25), channel_id=1, source_target_pairs={{0,2},{2,0},{1,3},{3,1},{4,6},{6,4},{5,7},{7,5},{8,10},{10,8},{9,1... | collective-permute-start | bytes 786440 | tf_op jit(solution)/shard_map/ppermute | solution.py:112
  89.0 7.5 %collective-permute-start = (f32[512,128]{1,0:T(8,128)S(1)}, f32[512,128]{1,0:T(8,128)S(1)}, u32[]{:S(2)}, u32[]{:S(2)}) collective-permute-start(f32[512,128]{1,0:T(8,128)S(1)} %bitcast.24), channel_id=1, source_target_pairs={{0,1},{1,0},{2,3},{3,2},{4,5},{5,4},{6,7},{7,6},{8,9},{9,8},{10,11... | collective-permute-start | bytes 786440 | tf_op jit(solution)/shard_map/ppermute | solution.py:110
  91.6 10.7 %collective-permute-start.1 = (f32[512,128]{1,0:T(8,128)S(1)}, f32[512,128]{1,0:T(8,128)S(1)}, u32[]{:S(2)}, u32[]{:S(2)}) collective-permute-start(f32[512,128]{1,0:T(8,128)S(1)} %bitcast.23), channel_id=1, source_target_pairs={{0,3},{3,0},{1,2},{2,1},{4,7},{7,4},{5,6},{6,5},{8,11},{11,8},{9,1... | collective-permute-start | bytes 786440 | tf_op jit(solution)/shard_map/ppermute | solution.py:111
  152.1 4.0 %collective-permute-start.3 = (f32[1024,128]{1,0:T(8,128)S(1)}, f32[1024,128]{1,0:T(8,128)S(1)}, u32[]{:S(2)}, u32[]{:S(2)}) collective-permute-start(f32[1024,128]{1,0:T(8,128)S(1)} %all_gather.15), channel_id=1, source_target_pairs={{0,1},{1,0},{2,3},{3,2},{4,5},{5,4},{6,7},{7,6},{8,9},{9,8},{10,11... | collective-permute-start | bytes 1572872 | tf_op jit(solution)/shard_map/ppermute | solution.py:124
